TPU v7x, 128 devices: a whole 4x4x4 slice. The times are simulated.
128 devices in a mesh: lat: 8 (over x, core), lev: 16 (over y, z).
Axes of the slice: x: 4, y: 4, z: 4, core: 2. Of those that a mesh axis runs over, the one named last changes fastest.
Arguments:
- spectral: float32 [2, 128, 256, 256], P(None, 'lev', 'lat'), may hold values from -6 to 6
- background: bfloat16 [384, 768, 128], P('lat', 'lev'), may hold values from -6 to 6
- columns: int32 [128, 2048], P(('lat', 'lev')), may hold values from 0 to 2303
- counts: int32 [128], P(('lat', 'lev')), may hold values from 1 to 2048, 131072 in all
- radiances: bfloat16 [128, 2048, 512], P(('lat', 'lev')), may hold values from -6 to 6
- used_pairs: int32 [128, 2048], P(('lat', 'lev')), may hold values from 1 to 256
- channel_weight: float32 [512], replicated, may hold values from 0.25 to 4
- weight_in: bfloat16 [128, 1024], replicated, may hold values from -0.5 to 0.5
- weight_mid: bfloat16 [1024, 1024], replicated, may hold values from -0.1875 to 0.1875
- weight_out: bfloat16 [1024, 512], replicated, may hold values from -0.1875 to 0.1875
Outputs:
- spectral_grad: float32 [2, 128, 256, 256], P(None, 'lev', 'lat')
- grid_grad: float32 [384, 768, 128], P('lat', 'lev')
Inputs may be any that keep to these rules, and one draw needn't show every extreme that they name: Entry [o, s] is the column of owner o's slot s inside o's region of 48 x 48 columns, numbered latitude-major; slots at or past counts[o] are unused. The counts sum to 131072, and the largest is exactly 2048. Block [o, s] uses channels 0 to 2 x used_pairs[o, s] - 1.
All inputs are finite; a program needn't handle non-finite values. No bound on the sum of `counts` on one device may be relied on, other than what follows from the above.
Results may differ from a plain program's by a relative error of at most 0.008.
Values may be sent and summed in bfloat16 or wider, within the bound.
No kernel may reach another device: no remote copies, remote signals or barrier semaphores. Data moves between devices by JAX's collectives and lax.ppermute only.
A program may use at most 128 MiB of HBM per device.

v0:
```python
import math
import jax
import jax.numpy as jnp
from jax import lax
from jax.sharding import PartitionSpec as P

M = 256
N = 256
NLAT = 384
NLON = 768
BLK_DEV = 1024
RESCALE_TOP = 2.0**60
RESCALE_BY = 2.0 ** (-60)
RESCALE_LOG = 60.0 * math.log(2.0)
HALF_LOG = 0.5 * math.log(0.5)


def shortened(shard):
    return jax.tree.map(lambda a: a.astype(jnp.bfloat16) if a.dtype == jnp.float32 else a, shard)


def legendre_table(orders, lat_total, degree_total):
    m_float = orders.astype(jnp.float32)
    lat_ids = jnp.arange(lat_total, dtype=jnp.float32)
    latitude = (0.5 - (lat_ids + 0.5) / lat_total) * jnp.pi
    sin_lat = jnp.sin(latitude)
    cos_lat = jnp.cos(latitude)
    order_ids = jnp.arange(1, degree_total, dtype=jnp.float32)
    log_steps = 0.5 * jnp.log((2.0 * order_ids + 1.0) / (2.0 * order_ids))
    log_norm = jnp.sum(
        jnp.where(order_ids[None, :] <= m_float[:, None], log_steps[None, :], 0.0), axis=1
    )
    log_start = HALF_LOG + log_norm[:, None] + m_float[:, None] * jnp.log(cos_lat)[None, :]

    def advance(recur_state, degree):
        previous, earlier, shifts = recur_state
        n_float = degree.astype(jnp.float32)
        on_diagonal = (n_float == m_float)[:, None]
        next_diag = (n_float == m_float + 1.0)[:, None]
        beyond = (n_float > m_float + 1.0)[:, None]
        factor_a = jnp.sqrt(
            jnp.maximum(4.0 * n_float * n_float - 1.0, 1.0)
            / jnp.maximum(n_float * n_float - m_float * m_float, 1.0)
        )
        lower = n_float - 1.0
        factor_b = jnp.sqrt(
            jnp.maximum(lower * lower - m_float * m_float, 0.0)
            / jnp.maximum(4.0 * lower * lower - 1.0, 1.0)
        )
        current = jnp.where(
            beyond,
            factor_a[:, None] * (sin_lat[None, :] * previous - factor_b[:, None] * earlier),
            0.0,
        )
        current = jnp.where(
            next_diag, jnp.sqrt(2.0 * m_float + 3.0)[:, None] * sin_lat[None, :] * previous, current
        )
        current = jnp.where(on_diagonal, 1.0, current)
        oversized = jnp.abs(current) > RESCALE_TOP
        current = jnp.where(oversized, current * RESCALE_BY, current)
        previous = jnp.where(oversized, previous * RESCALE_BY, previous)
        shifts = shifts + oversized.astype(jnp.float32)
        values = current * jnp.exp(log_start + shifts * RESCALE_LOG)
        return ((current, previous, shifts), values)

    zeros = jnp.zeros((orders.shape[0], lat_total), jnp.float32)
    _, legendre = lax.scan(
        advance, (zeros, zeros, zeros), jnp.arange(degree_total, dtype=jnp.int32), unroll=8
    )
    return legendre


def wave_table(wave_total, lon_total):
    wave_ids = jnp.arange(wave_total, dtype=jnp.int32)
    lon_ids = jnp.arange(lon_total, dtype=jnp.int32)
    phase = (wave_ids[:, None] * lon_ids[None, :] % lon_total).astype(jnp.float32) * (
        2.0 * math.pi / lon_total
    )
    weights = jnp.where(wave_ids == 0, 1.0, 2.0).astype(jnp.float32) / wave_total
    return jnp.stack([weights[:, None] * jnp.cos(phase), -weights[:, None] * jnp.sin(phase)])


def silu_slope(inputs):
    sigmoid_v = jax.nn.sigmoid(inputs)
    return sigmoid_v * (1.0 + inputs * (1.0 - sigmoid_v))


def radiance_pass(
    profiles, observed, pair_counts, usable, channel_weight, weight_in, weight_mid, weight_out
):
    pre_first = jnp.dot(profiles, weight_in, preferred_element_type=jnp.float32)
    act_first = jax.nn.silu(pre_first).astype(jnp.bfloat16)
    pre_second = jnp.dot(act_first, weight_mid, preferred_element_type=jnp.float32)
    act_second = jax.nn.silu(pre_second).astype(jnp.bfloat16)
    evolved = jnp.dot(act_second, weight_out, preferred_element_type=jnp.float32)
    channel_ids = jnp.arange(weight_out.shape[1], dtype=jnp.float32)
    active = (channel_ids[None, :] < 2.0 * pair_counts[:, None]) & usable[:, None]
    misfit = jnp.where(
        active, channel_weight[None, :] * (evolved - observed.astype(jnp.float32)), 0.0
    ).astype(jnp.bfloat16)
    back_second = (
        jnp.dot(misfit, weight_out.T, preferred_element_type=jnp.float32) * silu_slope(pre_second)
    ).astype(jnp.bfloat16)
    back_first = (
        jnp.dot(back_second, weight_mid.T, preferred_element_type=jnp.float32)
        * silu_slope(pre_first)
    ).astype(jnp.bfloat16)
    return jnp.dot(back_first, weight_in.T, preferred_element_type=jnp.float32).astype(jnp.bfloat16)


def route_out(profile_slots, observed_slots, pair_slots):
    arrived = (
        lax.all_to_all(profile_slots, ("lat", "lev"), split_axis=1, concat_axis=1, tiled=True),
        lax.all_to_all(observed_slots, ("lat", "lev"), split_axis=1, concat_axis=1, tiled=True),
        lax.all_to_all(pair_slots, ("lat", "lev"), split_axis=1, concat_axis=1, tiled=True),
    )
    return arrived


def route_back(reply):
    returned = lax.all_to_all(reply, ("lat", "lev"), split_axis=1, concat_axis=1, tiled=True)
    return returned


def dealt(
    profiles,
    observed,
    pair_counts,
    usable,
    counts,
    own_index,
    lat_count,
    lev_count,
    channel_weight,
    weight_in,
    weight_mid,
    weight_out,
):
    devices = lat_count * lev_count
    all_counts = lax.all_gather(counts, ("lat", "lev"), axis=0, tiled=True)
    start_ranks = jnp.cumsum(all_counts) - all_counts
    owner_ids = jnp.arange(devices, dtype=jnp.int32)
    own_start = jnp.sum(jnp.where(owner_ids == own_index, start_ranks, 0))
    lead_pos = own_start % devices
    capacity = profiles.shape[0]
    slot_count = (capacity + 2 * devices - 2) // devices

    def place(rows):
        keep = usable.reshape((capacity,) + (1,) * (rows.ndim - 1))
        masked = jnp.where(keep, rows, jnp.zeros((), rows.dtype))
        frame = jnp.zeros((slot_count * devices,) + rows.shape[1:], rows.dtype)
        frame = lax.dynamic_update_slice_in_dim(frame, masked, lead_pos, 0)
        return frame.reshape((slot_count, devices) + rows.shape[1:])

    arrived = route_out(place(profiles), place(observed), place(pair_counts.astype(jnp.bfloat16)))
    flat_profiles = arrived[0].reshape(slot_count * devices, -1)
    flat_observed = arrived[1].reshape(slot_count * devices, -1)
    flat_pairs = arrived[2].reshape(slot_count * devices)
    row_ids = jnp.arange(BLK_DEV, dtype=jnp.int32)
    my_ranks = own_index + devices * row_ids
    covers = start_ranks[None, :] <= my_ranks[:, None]
    source = jnp.sum(covers.astype(jnp.int32), axis=1) - 1
    source_start = jnp.max(jnp.where(covers, start_ranks[None, :], 0), axis=1)
    flat_pos = (row_ids - source_start // devices) * devices + source
    worker_grad = radiance_pass(
        jnp.take(flat_profiles, flat_pos, axis=0),
        jnp.take(flat_observed, flat_pos, axis=0),
        jnp.take(flat_pairs, flat_pos, axis=0).astype(jnp.float32),
        jnp.ones((BLK_DEV,), jnp.bool_),
        channel_weight,
        weight_in,
        weight_mid,
        weight_out,
    )
    slot_ids = jnp.arange(slot_count, dtype=jnp.int32)
    position = slot_ids[:, None] * devices + own_index - (start_ranks % devices)[None, :]
    returned = (position >= 0) & (position < all_counts[None, :])
    target = jnp.clip(start_ranks[None, :] // devices + slot_ids[:, None], 0, BLK_DEV - 1)
    reply = jnp.take(worker_grad, target.reshape(-1), axis=0).reshape(
        slot_count, devices, worker_grad.shape[1]
    )
    reply = jnp.where(returned[:, :, None], reply, jnp.zeros((), jnp.bfloat16))
    back_rows = route_back(reply).reshape(slot_count * devices, -1)
    mine = lax.dynamic_slice_in_dim(back_rows, lead_pos, capacity, 0)
    return jnp.where(usable[:, None], mine, jnp.zeros((), jnp.bfloat16))


def per_device(
    spectral,
    background,
    columns,
    counts,
    radiances,
    used_pairs,
    channel_weight,
    weight_in,
    weight_mid,
    weight_out,
):
    highest = lax.Precision.HIGHEST
    lat_count = lax.axis_size("lat")
    lev_count = lax.axis_size("lev")
    lat_index = lax.axis_index("lat")
    lev_index = lax.axis_index("lev")
    own_index = lat_index * lev_count + lev_index
    waves_local = spectral.shape[2]
    orders = lat_index * waves_local + jnp.arange(waves_local, dtype=jnp.int32)
    legendre = legendre_table(orders, NLAT, N)
    fourier = jnp.einsum("nmj,clmn->clmj", legendre, spectral, precision=highest)
    fourier = lax.all_to_all(fourier, "lat", split_axis=3, concat_axis=2, tiled=True)
    dft_table = wave_table(M, NLON)
    increment = jnp.einsum("clmj,cmx->jlx", fourier, dft_table, precision=highest)
    increment = lax.all_to_all(increment, "lev", split_axis=2, concat_axis=1, tiled=True)
    increment = jnp.transpose(increment, (0, 2, 1))
    grid_state = (background.astype(jnp.float32) + increment).astype(jnp.bfloat16)
    band_rows = grid_state.shape[0]
    tile_cols = grid_state.shape[1]
    cell_rows = grid_state.reshape(band_rows * tile_cols, grid_state.shape[2])
    local_cols = columns[0]
    profiles = jnp.take(cell_rows, local_cols, axis=0)
    capacity = local_cols.shape[0]
    usable = jnp.arange(capacity, dtype=jnp.int32) < counts[0]
    observed = radiances[0]
    pair_counts = used_pairs[0].astype(jnp.float32)
    block_grad = dealt(
        profiles,
        observed,
        pair_counts,
        usable,
        counts,
        own_index,
        lat_count,
        lev_count,
        channel_weight,
        weight_in,
        weight_mid,
        weight_out,
    )
    grid_grad = (
        jnp.zeros(cell_rows.shape, jnp.float32).at[local_cols].add(block_grad.astype(jnp.float32))
    )
    grid_grad = grid_grad.reshape(band_rows, tile_cols, cell_rows.shape[1])
    grad_rows = lax.all_to_all(
        jnp.transpose(grid_grad, (0, 2, 1)).astype(jnp.bfloat16),
        "lev",
        split_axis=1,
        concat_axis=2,
        tiled=True,
    ).astype(jnp.float32)
    coeff_grad = jnp.einsum("jlx,cmx->clmj", grad_rows, dft_table, precision=highest)
    coeff_grad = lax.all_to_all(
        shortened(coeff_grad), "lat", split_axis=2, concat_axis=3, tiled=True
    ).astype(coeff_grad.dtype)
    spectral_grad = jnp.einsum("nmj,clmj->clmn", legendre, coeff_grad, precision=highest)
    return (spectral_grad, grid_grad)


def solution(mesh):
    in_specs = (
        P(None, "lev", "lat", None),
        P("lat", "lev", None),
        P(("lat", "lev"), None),
        P(("lat", "lev")),
        P(("lat", "lev"), None, None),
        P(("lat", "lev"), None),
        P(),
        P(),
        P(),
        P(),
    )
    out_specs = (P(None, "lev", "lat", None), P("lat", "lev", None))
    return jax.shard_map(
        per_device, mesh=mesh, in_specs=in_specs, out_specs=out_specs, check_vma=False
    )
```

profile of v0, /device:TPU:1, one launch (start us, length us, event | category | flops | bytes accessed | tf_op | source)
XLA Modules:
  0.0 645.3 jit_solution(7367198378319178831)
XLA Ops:
  1.0 258.0 %while.23 = (s32[]{:T(128)}, f32[32,384]{1,0:T(8,128)S(1)}, f32[32,384]{1,0:T(8,128)S(1)}, f32[32,384]{1,0:T(8,128)S(1)}, f32[32,8,32,384]{3,2,1,0:T(8,128)}, /*...) while((s32[]{:T(128)}, f32[32,384]{1,0:T(8,128)S(1)}, ...), condition=%wide.region_6.7_spmd.clone.clone.clone.clone, body=%wide.region_5.6_spmd.clone.clone.clone.clone.sunk | while | flops 3778274 | bytes 3127550 | solution.py:67
  40.5 0.8 bitcast_dynamic-update-slice_fusion.26
  113.0 0.8 bitcast_dynamic-update-slice_fusion.26
  169.5 0.8 bitcast_dynamic-update-slice_fusion.26
  259.0 14.5 %fusion.88 = f32[2,8,32,384]{3,1,0,2:T(8,128)S(1)} fusion(f32[256,32,384]{2,1,0:T(8,128)} %bitcast.226, f32[2,8,32,256]{3,2,1,0:T(8,128)S(1)} %copy-done.6), kind=kOutput, calls=%fused_computation.199 | convolution fusion | flops 603979776 | bytes 13893632
  273.5 2.2 copy.162
  275.8 3.6 reshape.978
  279.3 5.8 all-to-all-start.1
  285.9 69.5 %all-reduce = s32[128]{0:T(128)S(1)} all-reduce(s32[128]{0:T(128)S(1)} %dynamic-update-slice), channel_id=1, replica_groups=mesh['lat'=8,'lev'=16] {'lat','lev'}, use_global_device_ids=true, to_apply=%add | all-reduce | flops 128 | bytes 1024
  359.9 4.1 sine_multiply_fusion
  364.0 5.0 all-to-all-start
  369.5 3.6 reduce.5
  373.2 3.8 reshape.979
  377.0 5.4 copy.208
  382.3 3.1 all_to_all.72
  385.5 3.7 convolution_bitcast_fusion
  389.2 2.3 copy.165
  391.5 5.1 reshape.980
  396.6 7.6 %all-to-all-start.2 = ((f32[16,1,18432]{2,1,0:T(1,128)}), f32[16,1,18432]{2,1,0:T(1,128)S(1)}, u32[]{:S(2)}, u32[]{:S(2)}) async-start(f32[16,1,18432]{2,1,0:T(1,128)} %reshape.980), calls=%async_computation.2 | async-start | bytes 2359296 | tf_op jit(solution)/shard_map/all_to_all | solution.py:213
  404.2 2.8 bitcast_select_fusion
  407.0 1.5 broadcast_in_dim.596
  408.5 11.3 %dynamic_update_slice.19 = bf16[2176,512]{1,0:T(8,128)(2,1)} dynamic-update-slice(bf16[2176,512]{1,0:T(8,128)(2,1)} %broadcast_in_dim.596, bf16[2048,512]{1,0:T(8,128)(2,1)} %bitcast_select_fusion, s32[]{:T(128)S(6)} %select_n.488, s32[]{:T(128)} %constant.254.clone.1) | dynamic-update-slice | bytes 4194308 | tf_op jit(solution)/shard_map/dynamic_update_slice | solution.py:152
  419.7 4.6 copy.170
  424.9 10.1 %all-to-all-start.4 = ((bf16[17,128,512]{2,0,1:T(8,128)(2,1)}), bf16[17,128,512]{2,0,1:T(8,128)(2,1)}, u32[]{:S(2)}, u32[]{:S(2)}) async-start(bf16[17,128,512]{2,0,1:T(8,128)(2,1)} %copy.170), calls=%async_computation.4 | async-start | bytes 6291456 | tf_op jit(solution)/shard_map/all_to_all | solution.py:114
  435.7 4.8 reduce.6
  440.4 3.6 reshape.981
  444.1 5.1 copy.166
  449.2 3.2 copy.167
  452.4 1.4 fusion.98
  453.8 6.2 gather_fusion.1
  460.0 2.3 select_select_fusion
  462.4 3.2 dynamic_update_slice.18
  465.5 1.3 copy.168
  466.8 8.5 %all-to-all-done.4 = bf16[17,128,512]{2,0,1:T(8,128)(2,1)} async-done(((bf16[17,128,512]{2,0,1:T(8,128)(2,1)}), bf16[17,128,512]{2,0,1:T(8,128)(2,1)}, u32[]{:S(2)}, u32[]{:S(2)}) %all-to-all-start.4) | async-done | bytes 2228256 | tf_op jit(solution)/shard_map/all_to_all | solution.py:114
  475.4 5.3 all-to-all-start.3
  482.0 6.8 %gather_fusion = bf16[1024]{0:T(1024)(128)(2,1)S(1)} fusion(bf16[2176]{0:T(1024)(128)(2,1)S(1)} %bitcast.224, s32[1024]{0:T(1024)S(1)} %broadcast_clamp_fusion.1), kind=kCustom, calls=%fused_computation | custom fusion | bytes 8192 | tf_op jit(solution)/shard_map/jit(_take)/gather | solution.py:168
  489.6 4.0 copy.171
  493.6 7.0 %gather_fusion.3 = bf16[1024,512]{1,0:T(8,128)(2,1)} fusion(bf16[2176,512]{1,0:T(8,128)(2,1)} %bitcast.225, s32[1024]{0:T(1024)S(1)} %broadcast_clamp_fusion.1), kind=kCustom, calls=%fused_computation.3 | custom fusion | bytes 2101248 | tf_op jit(solution)/shard_map/jit(_take)/gather | solution.py:167
  500.7 3.2 gather_fusion.2
  503.9 1.7 fusion.121
  505.7 4.3 fusion.85
  510.0 8.8 %multiply_convert_fusion.1 = bf16[1024,1024]{1,0:T(8,128)(2,1)} fusion(f32[1024,1024]{1,0:T(8,128)} %fusion.85, bf16[1024,512]{1,0:T(8,128)(2,1)} %param.21, bf16[1024,512]{1,0:T(8,128)(2,1)S(1)} %copy-done.3, f32[512]{0:T(512)S(1)} %copy-done.16, f32[1024]{0:T(1024)S(1)} %get-tuple-element.400, pred[1024]{0:T(1024)(128)(4,1)S(1)} %get-tuple-element.401), kind=kOutput, calls=%fused_computation.185 | convolution fusion | flops 2165833728 | bytes 8395776 | tf_op jit(solution)/shard_map/dot_general | solution.py:102
  518.9 6.0 fusion.97
  524.9 4.8 gather_fusion.4
  529.7 1.8 fusion.108
  531.6 26.2 %all_to_all.96 = bf16[17,128,128]{2,0,1:T(8,128)(2,1)S(1)} all-to-all(bf16[17,128,128]{2,0,1:T(8,128)(2,1)S(1)} %fusion.108), channel_id=1, replica_groups=mesh['lat'=8,'lev'=16] {'lat','lev'}, dimensions={1} | all-to-all | bytes 1114112 | tf_op jit(solution)/shard_map/all_to_all | solution.py:121
  557.8 0.9 copy.173
  558.7 12.2 %scatter_custom_fusion = f32[2304,128]{1,0:T(8,128)S(1)} fusion(s32[2048]{0:T(1024)} %bitcast.249, f32[]{:T(128)} %constant.260.clone.1, bf16[2176,128]{1,0:T(8,128)(2,1)} %bitcast.245, s32[]{:T(128)S(6)} %select_n.488, s32[]{:T(128)} %constant.254.clone.1, pred[2048]{0:T(1024)(128)(4,1)S(1)} %copy-done.12, bf16[]{:T(256)} %constant.276.clone.1), kind=kCustom, calls=%fused_computation.208 | custom fusion | flops 786432 | bytes 1707524 | tf_op jit(solution)/shard_map/scatter-add | solution.py:240
  571.0 1.0 convert_bitcast_fusion
  572.0 2.7 copy.174
  574.7 4.2 reshape.982
  578.8 15.5 %all_to_all.97 = bf16[16,2,9216]{2,1,0:T(2,128)(2,1)} all-to-all(bf16[16,2,9216]{2,1,0:T(2,128)(2,1)} %reshape.982), channel_id=1, replica_groups=mesh['lat'=8,'lev'=16] {'lev'}, dimensions={0} | all-to-all | bytes 1179648 | tf_op jit(solution)/shard_map/all_to_all | solution.py:243
  594.3 3.3 reshape.983
  597.6 3.7 copy.176
  601.3 2.7 reshape.967
  604.0 3.0 fusion.96
  607.1 1.9 copy.177
  609.0 1.5 reshape.984
  610.5 13.3 %all_to_all.98 = bf16[8,2,12288]{2,1,0:T(2,128)(2,1)} all-to-all(bf16[8,2,12288]{2,1,0:T(2,128)(2,1)S(1)} %reshape.984), channel_id=1, replica_groups=mesh['lat'=8,'lev'=16] {'lat'}, dimensions={0} | all-to-all | bytes 786432 | tf_op jit(solution)/shard_map/all_to_all | solution.py:251
  623.9 2.3 reshape.985
  626.1 2.3 copy.179
  628.4 2.0 all_to_all.87
  630.4 13.3 %fusion.93 = f32[2,8,32,256]{3,1,0,2:T(8,128)S(1)} fusion(bf16[2,8,32,384]{3,1,0,2:T(8,128)(2,1)S(1)} %all_to_all.87, f32[256,32,384,1]{2,1,0,3:T(8,128)} %bitcast.227), kind=kOutput, calls=%fused_computation.202 | convolution fusion | flops 603979776 | bytes 13500416 | tf_op jit(solution)/shard_map/nmj,clmj->clmn/dot_general | solution.py:254
  643.8 1.1 copy.181
  (1169 shorter events, 99.1 us)
Async XLA Ops:
  0.6 505.0 %copy-start = (bf16[1024,1024]{1,0:T(8,128)(2,1)S(1)}, bf16[1024,1024]{1,0:T(8,128)(2,1)}, u32[]{:S(2)}) copy-start(bf16[1024,1024]{1,0:T(8,128)(2,1)} %param.20) | copy-start | bytes 6291460
  1.0 258.1 %copy-start.6 = (f32[2,8,32,256]{3,2,1,0:T(8,128)S(1)}, f32[2,8,32,256]{3,2,1,0:T(8,128)}, u32[]{:S(2)}) copy-start(f32[2,8,32,256]{3,2,1,0:T(8,128)} %param.12) | copy-start | bytes 1572868
  275.8 82.7 %copy-start.15 = (s32[1,2048]{1,0:T(1,128)S(1)}, s32[1,2048]{1,0:T(1,128)}, u32[]{:S(2)}) copy-start(s32[1,2048]{1,0:T(1,128)} %param.17) | copy-start | bytes 24580
  279.3 84.7 %all-to-all-start.1 = ((f32[8,1,24576]{2,1,0:T(1,128)}), f32[8,1,24576]{2,1,0:T(1,128)S(1)}, u32[]{:S(2)}, u32[]{:S(2)}) async-start(f32[8,1,24576]{2,1,0:T(1,128)} %reshape.978), calls=%async_computation.1 | async-start | bytes 1572864 | tf_op jit(solution)/shard_map/all_to_all | solution.py:210
  364.0 32.6 %all-to-all-start = ((bf16[17,128,1]{0,2,1:T(2,128)(2,1)}), bf16[17,128,1]{0,2,1:T(2,128)(2,1)S(1)}, u32[]{:S(2)}, u32[]{:S(2)}) async-start(bf16[17,128,1]{0,2,1:T(2,128)(2,1)} %copy.158), calls=%async_computation | async-start | bytes 131072 | tf_op jit(solution)/shard_map/all_to_all | solution.py:115
  396.6 28.3 %all-to-all-start.2 = ((f32[16,1,18432]{2,1,0:T(1,128)}), f32[16,1,18432]{2,1,0:T(1,128)S(1)}, u32[]{:S(2)}, u32[]{:S(2)}) async-start(f32[16,1,18432]{2,1,0:T(1,128)} %reshape.980), calls=%async_computation.2 | async-start | bytes 2359296 | tf_op jit(solution)/shard_map/all_to_all | solution.py:213
  404.2 55.8 %copy-start.11 = (pred[2048]{0:T(1024)(128)(4,1)}, pred[2048]{0:T(1024)(128)(4,1)S(1)}, u32[]{:S(2)}) copy-start(pred[2048]{0:T(1024)(128)(4,1)S(1)} %iota_compare_fusion.1) | copy-start | bytes 6148
  424.8 10.2 %copy-start.10 = (s32[1024]{0:T(1024)}, s32[1024]{0:T(1024)S(1)}, u32[]{:S(2)}) copy-start(s32[1024]{0:T(1024)S(1)} %get-tuple-element.361) | copy-start | bytes 12292
  424.8 10.2 %copy-start.9 = (s32[1024]{0:T(1024)}, s32[1024]{0:T(1024)S(1)}, u32[]{:S(2)}) copy-start(s32[1024]{0:T(1024)S(1)} %get-tuple-element.360) | copy-start | bytes 12292
  424.8 10.2 %copy-start.13 = (s32[1,2048]{1,0:T(1,128)S(1)}, s32[1,2048]{1,0:T(1,128)}, u32[]{:S(2)}) copy-start(s32[1,2048]{1,0:T(1,128)} %param.14) | copy-start | bytes 24580
  424.9 50.5 %all-to-all-start.4 = ((bf16[17,128,512]{2,0,1:T(8,128)(2,1)}), bf16[17,128,512]{2,0,1:T(8,128)(2,1)}, u32[]{:S(2)}, u32[]{:S(2)}) async-start(bf16[17,128,512]{2,0,1:T(8,128)(2,1)} %copy.170), calls=%async_computation.4 | async-start | bytes 6291456 | tf_op jit(solution)/shard_map/all_to_all | solution.py:114
  435.7 8.4 %copy-start.14 = (s32[2048,1]{0,1:T(1,128)}, s32[2048,1]{0,1:T(1,128)S(1)}, u32[]{:S(2)}) copy-start(s32[2048,1]{0,1:T(1,128)S(1)} %compare_select_fusion.2) | copy-start | bytes 24580
  449.2 3.2 copy-start.5
  475.4 25.3 %all-to-all-start.3 = ((bf16[17,128,128]{2,0,1:T(8,128)(2,1)}), bf16[17,128,128]{2,0,1:T(8,128)(2,1)S(1)}, u32[]{:S(2)}, u32[]{:S(2)}) async-start(bf16[17,128,128]{2,0,1:T(8,128)(2,1)} %copy.168), calls=%async_computation.3 | async-start | bytes 1572864 | tf_op jit(solution)/shard_map/all_to_all | solution.py:113
  505.7 4.4 copy-start.2
  505.7 4.4 copy-start.3
  505.7 4.3 copy-start.16
  510.0 8.8 %copy-start.7 = (bf16[128,1024]{1,0:T(8,128)(2,1)S(1)}, bf16[128,1024]{1,0:T(8,128)(2,1)}, u32[]{:S(2)}) copy-start(bf16[128,1024]{1,0:T(8,128)(2,1)} %param.19) | copy-start | bytes 786436
  518.9 6.0 copy-start.8
  529.7 29.0 %copy-start.12 = (pred[2048]{0:T(1024)(128)(4,1)S(1)}, pred[2048]{0:T(1024)(128)(4,1)}, u32[]{:S(2)}) copy-start(pred[2048]{0:T(1024)(128)(4,1)} %copy-done.11) | copy-start | bytes 6148
  571.0 23.3 %copy-start.1 = (f32[2304,128]{1,0:T(8,128)}, f32[2304,128]{1,0:T(8,128)S(1)}, u32[]{:S(2)}) copy-start(f32[2304,128]{1,0:T(8,128)S(1)} %scatter_custom_fusion) | copy-start | bytes 3538948
  597.6 6.4 copy-start.4
where the time goes:
time: 658 us; the launch traced here: 645 us
  local copies, waits for them, and re-layouts  170 us (26%)
  loops' own time  163 us (25%)
  blocking collectives  125 us (19%)
  other arithmetic  85.6 us (13%)
  matrix products  55.4 us (8%)
  starting transfers between devices  33.7 us (5%)
  waiting for transfers between devices  8.55 us (1%)
    another operation x1, loops' own time, legendre_table(): lax.scan(advance, (zeros, zeros, zeros), jnp.arange(degree_total, dtype=j...  163 us
    unnamed x1, blocking collectives  69.5 us
    while x224, other arithmetic  31.7 us
    unnamed x45, local copies, waits for them, and re-layouts  28.7 us
    all_to_all x1, blocking collectives, route_back(): lax.all_to_all(reply, ('lat', 'lev'), split_axis=1, concat_axis=1, tiled=...  26.2 us
    dynamic_update_slice x32, local copies, waits for them, and re-layouts, legendre_table(): lax.scan(advance, (zeros, zeros, zeros), jnp.arange(degree_total, dtype=j...  25.3 us
    slice x32, local copies, waits for them, and re-layouts, legendre_table(): lax.scan(advance, (zeros, zeros, zeros), jnp.arange(degree_total, dtype=j...  19.7 us
    all_to_all x1, blocking collectives, per_device(): lax.all_to_all(jnp.transpose(grid_grad, (0, 2, 1)).astype(jnp.bfloat16),...  15.5 us
  transfers between devices with their start and end apart: 5, of which 1 were waited for; matrix products, arithmetic and copies ran while one was open for 16% of the time, Pallas kernels for 0%

commit v1 on v0

--- a/solution.py
+++ b/solution.py
@@ -248,9 +248,19 @@
         tiled=True,
     ).astype(jnp.float32)
     coeff_grad = jnp.einsum("jlx,cmx->clmj", grad_rows, dft_table, precision=highest)
-    coeff_grad = lax.all_to_all(
-        shortened(coeff_grad), "lat", split_axis=2, concat_axis=3, tiled=True
-    ).astype(coeff_grad.dtype)
+
+    def _pass_lane(array_here):
+        return jnp.concatenate(
+            lax.all_to_all(
+                jnp.stack(jnp.split(array_here, lax.axis_size("lat"), 2), 0),
+                "lat",
+                split_axis=0,
+                concat_axis=0,
+            ),
+            3,
+        )
+
+    coeff_grad = _pass_lane(shortened(coeff_grad)).astype(coeff_grad.dtype)
     spectral_grad = jnp.einsum("nmj,clmj->clmn", legendre, coeff_grad, precision=highest)
     return (spectral_grad, grid_grad)
 

time: 658 us -> 665 us (1.011)
    unnamed x45 -> x56, local copies, waits for them, and re-layouts: 28.7 us -> 34.1 us
where the time goes in v1:
time: 665 us; the launch traced here: 653 us
  local copies, waits for them, and re-layouts  175 us (26%)
  loops' own time  167 us (25%)
  blocking collectives  125 us (19%)
  other arithmetic  85 us (13%)
  matrix products  54.6 us (8%)
  starting transfers between devices  33.7 us (5%)
  waiting for transfers between devices  8.56 us (1%)
    another operation x1, loops' own time, legendre_table(): lax.scan(advance, (zeros, zeros, zeros), jnp.arange(degree_total, dtype=j...  167 us
    unnamed x1, blocking collectives  69.5 us
    unnamed x56, local copies, waits for them, and re-layouts  34.1 us
    while x224, other arithmetic  31.7 us
    all_to_all x1, blocking collectives, route_back(): lax.all_to_all(reply, ('lat', 'lev'), split_axis=1, concat_axis=1, tiled=...  26.3 us
    dynamic_update_slice x32, local copies, waits for them, and re-layouts, legendre_table(): lax.scan(advance, (zeros, zeros, zeros), jnp.arange(degree_total, dtype=j...  25.3 us
    slice x32, local copies, waits for them, and re-layouts, legendre_table(): lax.scan(advance, (zeros, zeros, zeros), jnp.arange(degree_total, dtype=j...  19.4 us
    all_to_all x1, blocking collectives, per_device(): lax.all_to_all(jnp.transpose(grid_grad, (0, 2, 1)).astype(jnp.bfloat16),...  15.4 us
  transfers between devices with their start and end apart: 5, of which 1 were waited for; matrix products, arithmetic and copies ran while one was open for 16% of the time, Pallas kernels for 0%

profile of v1, /device:TPU:1, one launch (start us, length us, event | category | flops | bytes accessed | tf_op | source)
XLA Modules:
  0.0 652.9 jit_solution(18408877598687010271)
XLA Ops:
  1.0 261.6 %while.23 = (s32[]{:T(128)}, f32[32,384]{1,0:T(8,128)S(1)}, f32[32,384]{1,0:T(8,128)S(1)}, f32[32,384]{1,0:T(8,128)S(1)}, f32[32,8,32,384]{3,2,1,0:T(8,128)}, /*...) while((s32[]{:T(128)}, f32[32,384]{1,0:T(8,128)S(1)}, ...), condition=%wide.region_6.7_spmd.clone.clone.clone.clone, body=%wide.region_5.6_spmd.clone.clone.clone.clone.sunk | while | flops 3778274 | bytes 3127550 | solution.py:67
  41.1 0.8 bitcast_dynamic-update-slice_fusion.26
  171.8 0.8 bitcast_dynamic-update-slice_fusion.26
  180.0 0.8 bitcast_dynamic-update-slice_fusion.26
  262.5 14.5 %fusion.88 = f32[2,8,32,384]{3,1,0,2:T(8,128)S(1)} fusion(f32[256,32,384]{2,1,0:T(8,128)} %bitcast.253, f32[2,8,32,256]{3,2,1,0:T(8,128)S(1)} %copy-done.6), kind=kOutput, calls=%fused_computation.199 | convolution fusion | flops 603979776 | bytes 13893632
  277.0 2.3 copy.163
  279.3 3.6 reshape.987
  282.8 5.8 all-to-all-start.1
  289.4 69.5 %all-reduce = s32[128]{0:T(128)S(1)} all-reduce(s32[128]{0:T(128)S(1)} %dynamic-update-slice), channel_id=1, replica_groups=mesh['lat'=8,'lev'=16] {'lat','lev'}, use_global_device_ids=true, to_apply=%add | all-reduce | flops 128 | bytes 1024
  363.5 4.1 sine_multiply_fusion
  367.6 5.0 all-to-all-start
  373.0 3.6 reduce.5
  376.7 3.8 reshape.988
  380.5 5.4 copy.209
  385.9 3.1 all_to_all.62
  389.0 3.7 convolution_bitcast_fusion
  392.7 2.3 copy.166
  395.0 5.1 reshape.989
  400.1 7.6 %all-to-all-start.2 = ((f32[16,1,18432]{2,1,0:T(1,128)}), f32[16,1,18432]{2,1,0:T(1,128)S(1)}, u32[]{:S(2)}, u32[]{:S(2)}) async-start(f32[16,1,18432]{2,1,0:T(1,128)} %reshape.989), calls=%async_computation.2 | async-start | bytes 2359296 | tf_op jit(solution)/shard_map/all_to_all | solution.py:213
  407.7 2.7 bitcast_select_fusion
  410.5 1.5 broadcast_in_dim.596
  412.0 11.2 %dynamic_update_slice.19 = bf16[2176,512]{1,0:T(8,128)(2,1)} dynamic-update-slice(bf16[2176,512]{1,0:T(8,128)(2,1)} %broadcast_in_dim.596, bf16[2048,512]{1,0:T(8,128)(2,1)} %bitcast_select_fusion, s32[]{:T(128)S(6)} %select_n.488, s32[]{:T(128)} %constant.254.clone.1) | dynamic-update-slice | bytes 4194308 | tf_op jit(solution)/shard_map/dynamic_update_slice | solution.py:152
  423.2 4.6 copy.171
  428.4 10.1 %all-to-all-start.4 = ((bf16[17,128,512]{2,0,1:T(8,128)(2,1)}), bf16[17,128,512]{2,0,1:T(8,128)(2,1)}, u32[]{:S(2)}, u32[]{:S(2)}) async-start(bf16[17,128,512]{2,0,1:T(8,128)(2,1)} %copy.171), calls=%async_computation.4 | async-start | bytes 6291456 | tf_op jit(solution)/shard_map/all_to_all | solution.py:114
  439.2 4.8 reduce.6
  444.0 3.6 reshape.990
  447.6 5.1 copy.167
  452.7 3.2 copy.168
  455.9 1.4 fusion.98
  457.3 6.2 gather_fusion.1
  463.5 2.3 select_select_fusion
  465.9 3.2 dynamic_update_slice.18
  469.0 1.3 copy.169
  470.3 8.6 %all-to-all-done.4 = bf16[17,128,512]{2,0,1:T(8,128)(2,1)} async-done(((bf16[17,128,512]{2,0,1:T(8,128)(2,1)}), bf16[17,128,512]{2,0,1:T(8,128)(2,1)}, u32[]{:S(2)}, u32[]{:S(2)}) %all-to-all-start.4) | async-done | bytes 2228256 | tf_op jit(solution)/shard_map/all_to_all | solution.py:114
  478.9 5.3 all-to-all-start.3
  485.6 6.8 %gather_fusion = bf16[1024]{0:T(1024)(128)(2,1)S(1)} fusion(bf16[2176]{0:T(1024)(128)(2,1)S(1)} %bitcast.251, s32[1024]{0:T(1024)S(1)} %broadcast_clamp_fusion.1), kind=kCustom, calls=%fused_computation | custom fusion | bytes 8192 | tf_op jit(solution)/shard_map/jit(_take)/gather | solution.py:168
  492.4 4.0 copy.172
  496.5 7.0 %gather_fusion.3 = bf16[1024,512]{1,0:T(8,128)(2,1)} fusion(bf16[2176,512]{1,0:T(8,128)(2,1)} %bitcast.252, s32[1024]{0:T(1024)S(1)} %broadcast_clamp_fusion.1), kind=kCustom, calls=%fused_computation.3 | custom fusion | bytes 2101248 | tf_op jit(solution)/shard_map/jit(_take)/gather | solution.py:167
  503.6 3.2 gather_fusion.2
  506.8 1.7 fusion.121
  508.6 4.3 fusion.85
  512.9 8.8 %multiply_convert_fusion.1 = bf16[1024,1024]{1,0:T(8,128)(2,1)} fusion(f32[1024,1024]{1,0:T(8,128)} %fusion.85, bf16[1024,512]{1,0:T(8,128)(2,1)} %param.21, bf16[1024,512]{1,0:T(8,128)(2,1)S(1)} %copy-done.3, f32[512]{0:T(512)S(1)} %copy-done.18, f32[1024]{0:T(1024)S(1)} %get-tuple-element.400, pred[1024]{0:T(1024)(128)(4,1)S(1)} %get-tuple-element.401), kind=kOutput, calls=%fused_computation.185 | convolution fusion | flops 2165833728 | bytes 8395776 | tf_op jit(solution)/shard_map/dot_general | solution.py:102
  521.7 6.0 fusion.97
  527.7 4.8 gather_fusion.4
  532.6 1.8 fusion.108
  534.4 26.3 %all_to_all.83 = bf16[17,128,128]{2,0,1:T(8,128)(2,1)S(1)} all-to-all(bf16[17,128,128]{2,0,1:T(8,128)(2,1)S(1)} %fusion.108), channel_id=1, replica_groups=mesh['lat'=8,'lev'=16] {'lat','lev'}, dimensions={1} | all-to-all | bytes 1114112 | tf_op jit(solution)/shard_map/all_to_all | solution.py:121
  560.7 0.9 copy.174
  561.6 12.2 %scatter_custom_fusion = f32[2304,128]{1,0:T(8,128)S(1)} fusion(s32[2048]{0:T(1024)} %bitcast.275, f32[]{:T(128)} %constant.260.clone.1, bf16[2176,128]{1,0:T(8,128)(2,1)} %bitcast.271, s32[]{:T(128)S(6)} %select_n.488, s32[]{:T(128)} %constant.254.clone.1, pred[2048]{0:T(1024)(128)(4,1)S(1)} %copy-done.14, bf16[]{:T(256)} %constant.276.clone.1), kind=kCustom, calls=%fused_computation.208 | custom fusion | flops 786432 | bytes 1707524 | tf_op jit(solution)/shard_map/scatter-add | solution.py:240
  573.9 1.0 convert_bitcast_fusion
  574.9 2.6 copy.175
  577.5 4.2 reshape.991
  581.6 15.4 %all_to_all.84 = bf16[16,2,9216]{2,1,0:T(2,128)(2,1)} all-to-all(bf16[16,2,9216]{2,1,0:T(2,128)(2,1)} %reshape.991), channel_id=1, replica_groups=mesh['lat'=8,'lev'=16] {'lev'}, dimensions={0} | all-to-all | bytes 1179648 | tf_op jit(solution)/shard_map/all_to_all | solution.py:243
  597.1 3.4 reshape.992
  600.4 3.7 copy.177
  604.1 2.7 reshape.975
  606.8 2.3 fusion.96
  615.4 1.8 copy.178
  617.2 1.5 reshape.993
  618.7 13.3 %all_to_all.85 = bf16[8,2,12288]{2,1,0:T(2,128)(2,1)} all-to-all(bf16[8,2,12288]{2,1,0:T(2,128)(2,1)S(1)} %reshape.993), channel_id=1, replica_groups=mesh['lat'=8,'lev'=16] {'lat'}, dimensions={0} | all-to-all | bytes 786432 | tf_op jit(solution)/shard_map/all_to_all | solution.py:254
  632.0 2.3 reshape.994
  634.3 1.7 copy.187
  636.0 2.0 reshape.978
  638.0 13.3 %fusion.93 = f32[2,8,32,256]{3,1,0,2:T(8,128)S(1)} fusion(bf16[2,8,32,384]{3,1,0,2:T(8,128)(2,1)S(1)} %reshape.978, f32[256,32,384,1]{2,1,0,3:T(8,128)} %bitcast.254), kind=kOutput, calls=%fused_computation.202 | convolution fusion | flops 603979776 | bytes 13500416 | tf_op jit(solution)/shard_map/nmj,clmj->clmn/dot_general | solution.py:264
  651.4 1.1 copy.182
  (1181 shorter events, 104.3 us)
Async XLA Ops:
  0.6 507.9 %copy-start = (bf16[1024,1024]{1,0:T(8,128)(2,1)S(1)}, bf16[1024,1024]{1,0:T(8,128)(2,1)}, u32[]{:S(2)}) copy-start(bf16[1024,1024]{1,0:T(8,128)(2,1)} %param.20) | copy-start | bytes 6291460
  1.0 261.6 %copy-start.6 = (f32[2,8,32,256]{3,2,1,0:T(8,128)S(1)}, f32[2,8,32,256]{3,2,1,0:T(8,128)}, u32[]{:S(2)}) copy-start(f32[2,8,32,256]{3,2,1,0:T(8,128)} %param.12) | copy-start | bytes 1572868
  279.3 82.7 %copy-start.17 = (s32[1,2048]{1,0:T(1,128)S(1)}, s32[1,2048]{1,0:T(1,128)}, u32[]{:S(2)}) copy-start(s32[1,2048]{1,0:T(1,128)} %param.17) | copy-start | bytes 24580
  282.8 84.7 %all-to-all-start.1 = ((f32[8,1,24576]{2,1,0:T(1,128)}), f32[8,1,24576]{2,1,0:T(1,128)S(1)}, u32[]{:S(2)}, u32[]{:S(2)}) async-start(f32[8,1,24576]{2,1,0:T(1,128)} %reshape.987), calls=%async_computation.1 | async-start | bytes 1572864 | tf_op jit(solution)/shard_map/all_to_all | solution.py:210
  367.6 32.6 %all-to-all-start = ((bf16[17,128,1]{0,2,1:T(2,128)(2,1)}), bf16[17,128,1]{0,2,1:T(2,128)(2,1)S(1)}, u32[]{:S(2)}, u32[]{:S(2)}) async-start(bf16[17,128,1]{0,2,1:T(2,128)(2,1)} %copy.159), calls=%async_computation | async-start | bytes 131072 | tf_op jit(solution)/shard_map/all_to_all | solution.py:115
  400.1 28.2 %all-to-all-start.2 = ((f32[16,1,18432]{2,1,0:T(1,128)}), f32[16,1,18432]{2,1,0:T(1,128)S(1)}, u32[]{:S(2)}, u32[]{:S(2)}) async-start(f32[16,1,18432]{2,1,0:T(1,128)} %reshape.989), calls=%async_computation.2 | async-start | bytes 2359296 | tf_op jit(solution)/shard_map/all_to_all | solution.py:213
  407.7 55.7 %copy-start.13 = (pred[2048]{0:T(1024)(128)(4,1)}, pred[2048]{0:T(1024)(128)(4,1)S(1)}, u32[]{:S(2)}) copy-start(pred[2048]{0:T(1024)(128)(4,1)S(1)} %iota_compare_fusion.1) | copy-start | bytes 6148
  428.3 10.2 %copy-start.11 = (s32[1024]{0:T(1024)}, s32[1024]{0:T(1024)S(1)}, u32[]{:S(2)}) copy-start(s32[1024]{0:T(1024)S(1)} %get-tuple-element.361) | copy-start | bytes 12292
  428.3 10.2 %copy-start.9 = (s32[1024]{0:T(1024)}, s32[1024]{0:T(1024)S(1)}, u32[]{:S(2)}) copy-start(s32[1024]{0:T(1024)S(1)} %get-tuple-element.360) | copy-start | bytes 12292
  428.3 10.2 %copy-start.15 = (s32[1,2048]{1,0:T(1,128)S(1)}, s32[1,2048]{1,0:T(1,128)}, u32[]{:S(2)}) copy-start(s32[1,2048]{1,0:T(1,128)} %param.14) | copy-start | bytes 24580
  428.4 50.5 %all-to-all-start.4 = ((bf16[17,128,512]{2,0,1:T(8,128)(2,1)}), bf16[17,128,512]{2,0,1:T(8,128)(2,1)}, u32[]{:S(2)}, u32[]{:S(2)}) async-start(bf16[17,128,512]{2,0,1:T(8,128)(2,1)} %copy.171), calls=%async_computation.4 | async-start | bytes 6291456 | tf_op jit(solution)/shard_map/all_to_all | solution.py:114
  439.2 8.4 %copy-start.16 = (s32[2048,1]{0,1:T(1,128)}, s32[2048,1]{0,1:T(1,128)S(1)}, u32[]{:S(2)}) copy-start(s32[2048,1]{0,1:T(1,128)S(1)} %compare_select_fusion.2) | copy-start | bytes 24580
  452.7 3.2 copy-start.5
  470.3 22.1 %copy-start.10 = (s32[1024]{0:T(1024)S(1)}, s32[1024]{0:T(1024)}, u32[]{:S(2)}) copy-start(s32[1024]{0:T(1024)} %copy-done.9) | copy-start | bytes 12292
  470.3 22.1 %copy-start.12 = (s32[1024]{0:T(1024)S(1)}, s32[1024]{0:T(1024)}, u32[]{:S(2)}) copy-start(s32[1024]{0:T(1024)} %copy-done.11) | copy-start | bytes 12292
  478.9 24.6 %all-to-all-start.3 = ((bf16[17,128,128]{2,0,1:T(8,128)(2,1)}), bf16[17,128,128]{2,0,1:T(8,128)(2,1)S(1)}, u32[]{:S(2)}, u32[]{:S(2)}) async-start(bf16[17,128,128]{2,0,1:T(8,128)(2,1)} %copy.169), calls=%async_computation.3 | async-start | bytes 1572864 | tf_op jit(solution)/shard_map/all_to_all | solution.py:113
  508.6 4.4 copy-start.2
  508.6 4.4 copy-start.3
  508.6 4.3 copy-start.18
  512.9 8.8 %copy-start.7 = (bf16[128,1024]{1,0:T(8,128)(2,1)S(1)}, bf16[128,1024]{1,0:T(8,128)(2,1)}, u32[]{:S(2)}) copy-start(bf16[128,1024]{1,0:T(8,128)(2,1)} %param.19) | copy-start | bytes 786436
  521.7 6.0 copy-start.8
  532.5 29.1 %copy-start.14 = (pred[2048]{0:T(1024)(128)(4,1)S(1)}, pred[2048]{0:T(1024)(128)(4,1)}, u32[]{:S(2)}) copy-start(pred[2048]{0:T(1024)(128)(4,1)} %copy-done.13) | copy-start | bytes 6148
  573.8 7.8 %copy-start.1 = (f32[2304,128]{1,0:T(8,128)}, f32[2304,128]{1,0:T(8,128)S(1)}, u32[]{:S(2)}) copy-start(f32[2304,128]{1,0:T(8,128)S(1)} %scatter_custom_fusion) | copy-start | bytes 3538948
  600.4 6.4 copy-start.4
